TPU v7x, 128 devices: a whole 4x4x4 slice. The times are simulated.
128 devices in a mesh: row: 16 (over y, z), col: 8 (over x, core).
Axes of the slice: x: 4, y: 4, z: 4, core: 2. Of those that a mesh axis runs over, the one named last changes fastest.
Arguments:
- front: float32 [2, 8192, 4, 4096], P(None, 'row', None, 'col')
- child_blocks: float32 [2, 8192, 8192], P(None, 'row', 'col')
- index_maps: int32 [2, 8192], replicated, may hold values from 0 to 16383, as said below
Outputs:
- schur: float32 [2, 8192, 4, 4096], P(None, 'row', None, 'col')
- factor: float32 [2, 8192, 1024], P(None, 'row')
Inputs may be any that keep to these rules, and one draw needn't show every extreme that they name: Within one child the map names distinct front indices. Entry index_maps[h, (s * R + k) * 32 + i], with R the number of row indices, names an index in a block b of 512 indices with b mod R equal to k.
All inputs are finite; a program needn't handle non-finite values.
Results may differ from a plain program's by a relative error of at most 0.0001.
Values sent between devices are 32-bit elements; how exact they have to be, the bound alone decides.
A program may use at most 128 MiB of HBM per device.

v0:
```python
import jax
import jax.numpy as jnp
from jax import lax
from jax.sharding import PartitionSpec as P

NB = 512


def spread(value, axis, source):
    kept = jnp.where(lax.axis_index(axis) == source, value, 0).astype(value.dtype)
    return lax.psum(kept, axis)


def share_panel(values, root):
    return spread(values, "col", root)


def factor_panel(panel, section, my_row, row_count):
    pivot = spread(panel[:NB], "row", section)
    lower = jnp.linalg.cholesky(pivot)
    solved = lax.linalg.triangular_solve(
        lower, panel, left_side=False, lower=True, transpose_a=True
    )
    rows_local = panel.shape[0]
    block_ids = jnp.arange(rows_local, dtype=jnp.int32) // NB * row_count + my_row
    tiled = jnp.tile(lower, (rows_local // NB, 1))
    zeros = jnp.zeros_like(solved)
    picked = jnp.where((block_ids == section)[:, None], tiled, solved)
    return jnp.where((block_ids < section)[:, None], zeros, picked)


def column_rows(factor_rows, my_col, row_count, col_count):
    pieces = [
        spread(factor_rows, "row", my_col + turn * col_count)
        for turn in range(row_count // col_count)
    ]
    blocks = factor_rows.shape[0] // NB
    shaped = [piece.reshape(blocks, NB, NB) for piece in pieces]
    return jnp.stack(shaped, axis=1).reshape(-1, NB)


def outer_update(matrix, left_rows, right_rows):
    return matrix - jnp.dot(
        left_rows, right_rows.T, precision=lax.Precision.HIGHEST, preferred_element_type=jnp.float32
    )


def group_columns(blocks, row_count, col_count):
    children, height, width = blocks.shape
    ratio = row_count // col_count
    shaped = blocks.reshape(children, height, ratio, ratio, col_count, -1)
    return shaped.transpose(0, 1, 4, 2, 3, 5).reshape(children, height, width)


def local_position(global_ids, count):
    return global_ids // (NB * count) * NB + global_ids % NB


def inverse_map(positions, length):
    arriving = jnp.arange(positions.shape[0], dtype=jnp.int32)
    inverse = jnp.full((length,), -1, jnp.int32).at[positions].set(arriving)
    return (jnp.maximum(inverse, 0), inverse >= 0)


def on_device(front, child_blocks, index_maps):
    row_blocks, block_rows, col_blocks, block_cols = front.shape
    rows_local = row_blocks * block_rows
    cols_local = col_blocks * block_cols
    row_count = lax.axis_size("row")
    col_count = lax.axis_size("col")
    my_row = lax.axis_index("row")
    my_col = lax.axis_index("col")
    summed = front.reshape(rows_local, cols_local)
    outgoing = group_columns(child_blocks, row_count, col_count)
    arrived = lax.all_to_all(
        lax.all_to_all(outgoing, "row", split_axis=1, concat_axis=1, tiled=True),
        "col",
        split_axis=2,
        concat_axis=2,
        tiled=True,
    )
    children = child_blocks.shape[0]
    ratio = row_count // col_count
    row_ids = lax.dynamic_index_in_dim(
        index_maps.reshape(children, row_count, row_count, -1), my_row, 2, keepdims=False
    ).reshape(children, -1)
    col_ids = lax.dynamic_index_in_dim(
        index_maps.reshape(children, col_count, ratio, ratio, col_count, -1),
        my_col,
        4,
        keepdims=False,
    ).reshape(children, -1)
    local_rows = local_position(row_ids, row_count)
    local_cols = local_position(col_ids, col_count)
    for child in range(children):
        row_take, row_valid = inverse_map(local_rows[child], rows_local)
        col_take, col_valid = inverse_map(local_cols[child], cols_local)
        widened = jnp.where(col_valid[None, :], jnp.take(arrived[child], col_take, axis=1), 0.0)
        placed = jnp.where(row_valid[:, None], jnp.take(widened, row_take, axis=0), 0.0)
        summed = summed + placed
    panel = share_panel(summed[:, :NB], 0)
    outputs = []
    for section in range(2):
        factor_rows = factor_panel(panel, section, my_row, row_count)
        factor_cols = column_rows(factor_rows, my_col, row_count, col_count)
        summed = outer_update(summed, factor_rows, factor_cols)
        outputs.append(factor_rows)
        if section == 0:
            panel = share_panel(summed[:, :NB], 1)
    schur = summed.reshape(front.shape)
    factor = jnp.concatenate(outputs, axis=1).reshape(row_blocks, block_rows, 2 * NB)
    return (schur, factor)


def solution(mesh):
    placed = (P(None, "row", None, "col"), P(None, "row", "col"), P())
    return jax.shard_map(
        on_device,
        mesh=mesh,
        in_specs=placed,
        out_specs=(P(None, "row", None, "col"), P(None, "row", None)),
        check_vma=False,
    )
```

profile of v0, /device:TPU:115, one launch (start us, length us, event | category | flops | bytes accessed | tf_op | source)
XLA Modules:
  0.0 1172.3 jit_solution(15224041002027477895)
XLA Ops:
  24.8 53.2 %all_to_all.10 = f32[2,512,1024]{2,0,1:T(2,128)} all-to-all(f32[2,512,1024]{2,0,1:T(2,128)} %copy.68), channel_id=1, replica_groups=mesh['row'=16,'col'=8] {'row'}, dimensions={1} | all-to-all | bytes 8388608 | tf_op jit(solution)/shard_map/all_to_all | solution.py:76
  128.7 13.0 %all-to-all-done.1 = f32[2,512,1024]{1,0,2:T(2,128)} async-done(((f32[2,512,1024]{1,0,2:T(2,128)}), f32[2,512,1024]{1,0,2:T(2,128)}, u32[]{:S(2)}, u32[]{:S(2)}) %all-to-all-start.1) | async-done | bytes 4194336 | tf_op jit(solution)/shard_map/all_to_all | solution.py:75
  150.5 11.1 gather_fusion
  244.6 63.0 %all-reduce.10.cloned.1.call-done = f32[1024,512]{0,1:T(8,128)} async-done(((f32[1024,512]{0,1:T(8,128)}), f32[1024,512]{0,1:T(8,128)}) %all-reduce.10.cloned.1.call-update) | async-done | bytes 2097168 | tf_op jit(solution)/shard_map/psum | solution.py:11
  310.2 88.1 %all-reduce.12.cloned.1.call-done = f32[512,512]{0,1:T(8,128)} async-done(((f32[512,512]{0,1:T(8,128)}), f32[512,512]{0,1:T(8,128)}) %all-reduce.12.cloned.1.call-update) | async-done | bytes 1048592 | tf_op jit(solution)/shard_map/psum | solution.py:11
  400.3 11.7 cholesky.286
  422.6 11.7 cholesky.305
  446.5 11.7 cholesky.326
  469.3 11.7 cholesky.343
  486.0 11.9 %while.4 = (s32[]{:T(128)}, f32[512,512]{1,0:T(8,128)}, s32[4,2]{0,1:T(2,128)S(1)}, f32[4,128,128]{2,1,0:T(8,128)S(1)}, s32[]{:T(128)}) while((s32[]{:T(128)}, f32[512,512]{1,0:T(8,128)}, s32[4,2]{0,1:T(2,128)S(1)}, f32[4,128,128]{2,1,0:T(8,128)S(1)}, s32[]{:T(128)}) %tuple.76), condition=%wide.while_cond, body=%wide.while_body.sunk | while | flops 2 | bytes 131181 | solution.py:21
  497.9 39.3 %custom-call.30 = f32[4,128,128]{1,2,0:T(8,128)S(1)} custom-call(f32[4,128,128]{2,1,0:T(8,128)S(1)} %get-tuple-element.20), custom_call_target="InvertDiagBlocksLowerTriangular" | custom-call | tf_op jit(solution)/shard_map/triangular_solve/custom-call.3 | solution.py:21
  560.2 104.6 %all-reduce.20.cloned.1.call-done = (f32[2,1,512,512]{3,2,1,0:T(8,128)}, f32[2,1,512,512]{3,2,1,0:T(8,128)}) async-done(((f32[2,1,512,512]{3,2,1,0:T(8,128)}, f32[2,1,512,512]{3,2,1,0:T(8,128)}), (f32[2,1,512,512]{3,2,1,0:T(8,128)}, f32[2,1,512,512]{3,2,1,0:T(8,128)})) %all-reduce.20.cloned.1.call-update) | async-done | bytes 4194320 | tf_op jit(solution)/shard_map/psum | solution.py:11
  667.4 17.1 %convolution_subtract_fusion.1 = f32[1024,2048]{0,1:T(8,128)S(1)} fusion(f32[1024,2048]{0,1:T(8,128)} %copy-done.1, f32[1024,512]{0,1:T(8,128)S(1)} %get-tuple-element.55, f32[2048,512]{1,0:T(8,128)S(1)} %bitcast.156), kind=kOutput, calls=%fused_computation.22 | convolution fusion | flops 12886999040 | bytes 23068672 | tf_op jit(solution)/shard_map/dot_general | solution.py:43
  689.5 63.6 %all-reduce.14.cloned.1.call-done = f32[1024,512]{0,1:T(8,128)} async-done(((f32[1024,512]{0,1:T(8,128)}), f32[1024,512]{0,1:T(8,128)}) %all-reduce.14.cloned.1.call-update) | async-done | bytes 2097168 | tf_op jit(solution)/shard_map/psum | solution.py:11
  755.9 87.8 %all-reduce.16.cloned.1.call-done = f32[512,512]{0,1:T(8,128)} async-done(((f32[512,512]{0,1:T(8,128)}), f32[512,512]{0,1:T(8,128)}) %all-reduce.16.cloned.1.call-update) | async-done | bytes 1048592 | tf_op jit(solution)/shard_map/psum | solution.py:11
  848.7 11.7 cholesky.358
  873.0 11.7 cholesky.377
  897.5 11.7 cholesky.398
  921.2 11.7 cholesky.415
  949.0 39.3 %custom-call.34 = f32[4,128,128]{1,2,0:T(8,128)S(1)} custom-call(f32[4,128,128]{2,1,0:T(8,128)S(1)} %get-tuple-element.21), custom_call_target="InvertDiagBlocksLowerTriangular" | custom-call | tf_op jit(solution)/shard_map/triangular_solve/custom-call.3 | solution.py:21
  1024.1 95.4 %all-reduce.18.cloned.1.call-done = (f32[2,1,512,512]{3,2,1,0:T(8,128)}, f32[2,1,512,512]{3,2,1,0:T(8,128)}) async-done(((f32[2,1,512,512]{3,2,1,0:T(8,128)}, f32[2,1,512,512]{3,2,1,0:T(8,128)}), (f32[2,1,512,512]{3,2,1,0:T(8,128)}, f32[2,1,512,512]{3,2,1,0:T(8,128)})) %all-reduce.18.cloned.1.call-update) | async-done | bytes 4194320 | tf_op jit(solution)/shard_map/psum | solution.py:11
  1122.4 17.8 %convolution_subtract_fusion = f32[1024,2048]{0,1:T(8,128)} fusion(f32[1024,2048]{0,1:T(8,128)} %copy-done, f32[1024,512]{0,1:T(8,128)S(1)} %copy-done.3, f32[2048,512]{1,0:T(8,128)S(1)} %bitcast.155), kind=kOutput, calls=%fused_computation.21 | convolution fusion | flops 12886999040 | bytes 23068672 | tf_op jit(solution)/shard_map/dot_general | solution.py:43
  1140.2 11.7 reshape.242
  1151.9 13.2 %copy.92 = f32[2,512,4,512]{3,2,1,0:T(4,128)} copy(f32[2,512,4,512]{1,0,3,2:T(2,128)} %reshape.242) | data formatting | bytes 16777216
  (203 shorter events, 351.1 us)
Async XLA Ops:
  87.2 6.7 copy-start.15
  87.2 54.5 %all-to-all-start.1 = ((f32[2,512,1024]{1,0,2:T(2,128)}), f32[2,512,1024]{1,0,2:T(2,128)}, u32[]{:S(2)}, u32[]{:S(2)}) async-start(f32[2,512,1024]{1,0,2:T(2,128)} %copy.69), calls=%async_computation.1 | async-start | bytes 8388608 | tf_op jit(solution)/shard_map/all_to_all | solution.py:75
  93.9 213.7 %all-reduce.10.cloned.1.call-start = ((), (), s32[]{:S(2)}) async-start(), calls=%async_computation.2 | async-start | bytes 4194304 | tf_op jit(solution)/shard_map/psum | solution.py:11
  239.7 3.4 copy-start.1
  244.6 153.7 %all-reduce.12.cloned.1.call-start = ((), (), s32[]{:S(2)}) async-start(), calls=%async_computation.3 | async-start | bytes 2097152 | tf_op jit(solution)/shard_map/psum | solution.py:11
  309.9 354.8 %all-reduce.20.cloned.1.call-start = ((), (), s32[]{:S(2)}) async-start(), calls=%async_computation.7 | async-start | bytes 8388608 | tf_op jit(solution)/shard_map/psum | solution.py:11
  398.3 1.7 copy-start.10
  497.9 43.3 %copy-start.4 = (f32[1024,512]{0,1:T(8,128)S(1)}, f32[1024,512]{0,1:T(8,128)}, u32[]{:S(2)}) copy-start(f32[1024,512]{0,1:T(8,128)} %all-reduce.10.cloned.1.call-done) | copy-start | bytes 6291460
  543.5 2.3 copy-start.8
  549.5 1.0 copy-start.9
  549.5 1.2 copy-start.14
  559.9 193.2 %all-reduce.14.cloned.1.call-start = ((), (), s32[]{:S(2)}) async-start(), calls=%async_computation.4 | async-start | bytes 4194304 | tf_op jit(solution)/shard_map/psum | solution.py:11
  684.6 3.4 copy-start
  689.5 154.2 %all-reduce.16.cloned.1.call-start = ((), (), s32[]{:S(2)}) async-start(), calls=%async_computation.5 | async-start | bytes 2097152 | tf_op jit(solution)/shard_map/psum | solution.py:11
  755.4 364.1 %all-reduce.18.cloned.1.call-start = ((), (), s32[]{:S(2)}) async-start(), calls=%async_computation.6 | async-start | bytes 8388608 | tf_op jit(solution)/shard_map/psum | solution.py:11
  843.7 2.6 copy-start.11
  847.8 1.0 copy-start.12
  988.3 4.2 copy-start.5
  994.7 2.3 copy-start.6
  1002.9 1.0 copy-start.7
  1002.9 1.2 copy-start.13
  1006.0 1.3 copy-start.2
  1119.5 2.9 copy-start.3
Sparse Core Ops, SparseCore 0:
  244.7 62.8 all-reduce.9
  311.5 86.8 all-reduce.11
  560.0 104.6 all-reduce.19
  689.6 63.4 all-reduce.13
  756.8 86.8 all-reduce.15
  1014.8 104.6 all-reduce.17
where the time goes:
time: 1190 us; the launch traced here: 1170 us
  waiting for transfers between devices  516 us (43%)
  other arithmetic  284 us (24%)
  local copies, waits for them, and re-layouts  229 us (19%)
  matrix products  62.2 us (5%)
  blocking collectives  53.2 us (4%)
  between operations  20.3 us (2%)
    psum x6, waiting for transfers between devices, spread(): return lax.psum(kept, axis)  502 us
    another operation x30, other arithmetic, factor_panel(): lower = jnp.linalg.cholesky(pivot)  159 us
    another operation x5, other arithmetic, factor_panel(): lax.linalg.triangular_solve(lower, panel, left_side=False, lower=True, tr...  82.2 us
    all_to_all x1, blocking collectives, on_device(): lax.all_to_all(outgoing, 'row', split_axis=1, concat_axis=1, tiled=True)  53.2 us
    unnamed x38, local copies, waits for them, and re-layouts  46.2 us
    gather x4, local copies, waits for them, and re-layouts, on_device(): jnp.take(widened, row_take, axis=0)  40.6 us
    dot_general x2, matrix products, outer_update(): jnp.dot(left_rows, right_rows.T, precision=lax.Precision.HIGHEST, preferr...  34.9 us
  transfers between devices with their start and end apart: 7, of which 7 were waited for; matrix products, arithmetic and copies ran while one was open for 4% of the time, Pallas kernels for 0%

commit v1 on v0

v1 whole, which is shorter than its diff:
```python
import functools
import jax
import jax.numpy as jnp
from jax import lax
from jax.experimental import pallas as pl
from jax.experimental.pallas import tpu as pltpu
from jax.sharding import PartitionSpec as P

NB = 512
MESH = pl.DeviceIdType.MESH
BF = jnp.bfloat16
F32 = jnp.float32


def split3(value):
    first = value.astype(BF)
    rest = value - first.astype(F32)
    second = rest.astype(BF)
    third = (rest - second.astype(F32)).astype(BF)
    return first, second, third


def dot(left, right):
    return jnp.dot(left, right, preferred_element_type=F32)


def exchange_kernel(rows, cols, child_ref, front_ref, row_ids_ref, col_ids_ref, out_ref,
                    staged, grouped, received, summed, child_sem, front_sems, send_sems, recv_sem):
    my_row = lax.axis_index("row")
    my_col = lax.axis_index("col")
    loads = [
        pltpu.make_async_copy(child_ref, staged, child_sem)
    ]
    loads[0].start()
    for b in range(2):
        for q in range(4):
            pltpu.make_async_copy(
                front_ref.at[b, :, q, :],
                summed.at[pl.ds(b * NB, NB), pl.ds(q * NB, NB)],
                front_sems.at[b * 4 + q],
            ).start()
    loads[0].wait()

    def group_rows(k):
        lanes = lax.broadcasted_iota(jnp.int32, (32, 128), 1) // 32
        at = pl.ds(pl.multiple_of(k * 32, 32), 32)
        for h in range(2):
            tiles = [staged[h, at, t * 128:(t + 1) * 128] for t in range(8)]
            for dest in range(8):
                made = None
                for part in range(4):
                    source = tiles[part * 2 + dest // 4]
                    shift = (part * 32 - (dest % 4) * 32) % 128
                    moved = pltpu.roll(source, shift, axis=1) if shift else source
                    made = moved if made is None else jnp.where(lanes == part, moved, made)
                grouped[h, at, dest * 128:(dest + 1) * 128] = made

    def block(ref, row, col):
        return ref.at[
            :, pl.ds(pl.multiple_of(row * 32, 32), 32), pl.ds(pl.multiple_of(col * 128, 128), 128)
        ]

    def send(k, dest, sem):
        pltpu.make_async_remote_copy(
            src_ref=block(grouped, k, dest),
            dst_ref=block(received, my_row, my_col),
            send_sem=send_sems.at[sem],
            recv_sem=recv_sem,
            device_id=(k, dest),
            device_id_type=MESH,
        ).start()

    @pl.loop(0, rows)
    def _(t):
        k = lax.rem(my_row + t, rows)
        group_rows(k)
        for u in range(1, cols):
            send(k, lax.rem(my_col + u, cols), 0)

        @pl.when(t > 0)
        def _():
            send(k, my_col, 1)

    own = pltpu.make_async_copy(
        block(grouped, my_row, my_col), block(received, my_row, my_col), recv_sem
    )
    own.start()
    for b in range(2):
        for q in range(4):
            pltpu.make_async_copy(
                front_ref.at[b, :, q, :],
                summed.at[pl.ds(b * NB, NB), pl.ds(q * NB, NB)],
                front_sems.at[b * 4 + q],
            ).wait()
    pltpu.make_async_copy(received, received, recv_sem).wait()
    pltpu.make_async_copy(
        grouped.at[:, :, pl.ds(0, 896)], grouped.at[:, :, pl.ds(0, 896)], send_sems.at[0]
    ).wait()
    pltpu.make_async_copy(
        grouped.at[:, pl.ds(0, 480), pl.ds(0, 128)],
        grouped.at[:, pl.ds(0, 480), pl.ds(0, 128)],
        send_sems.at[1],
    ).wait()

    for h in range(2):
        pieces = [split3(received[h, r:r + 256, :]) for r in (0, 256)]
        stacked = jnp.concatenate([p for piece in pieces for p in piece], axis=0)
        row_map = (
            lax.broadcasted_iota(jnp.int32, (1024, 512), 0) == row_ids_ref[h:h + 1, :]
        ).astype(BF)

        @pl.loop(0, 8)
        def _(n):
            at = pl.ds(pl.multiple_of(n * 256, 256), 256)
            col_map = (
                lax.broadcasted_iota(jnp.int32, (1024, 256), 1) + n * 256 == col_ids_ref[h]
            ).astype(BF)
            wide = dot(stacked, col_map)
            total = summed[:, at]
            for half in range(2):
                base = half * 768
                value = (wide[base:base + 256] + wide[base + 256:base + 512]) + wide[base + 512:base + 768]
                for p in split3(value):
                    total += dot(row_map[:, half * 256:half * 256 + 256], p)
            summed[:, at] = total

    done = pltpu.make_async_copy(summed, out_ref, child_sem)
    done.start()
    done.wait()


def local_position(ids, count):
    return ids // (NB * count) * NB + ids % NB


def id_tables(index_maps, rows, cols):
    my_row = lax.axis_index("row")
    my_col = lax.axis_index("col")
    ratio = rows // cols
    row_ids = lax.dynamic_index_in_dim(
        index_maps.reshape(2, rows, rows, -1), my_row, 2, keepdims=False
    ).reshape(2, -1)
    col_ids = lax.dynamic_index_in_dim(
        index_maps.reshape(2, cols, ratio, ratio, cols, -1), my_col, 4, keepdims=False
    ).reshape(2, -1)
    return local_position(row_ids, rows), local_position(col_ids, cols)[:, :, None]


def exchange(front, child_blocks, index_maps, rows, cols):
    row_ids, col_ids = id_tables(index_maps, rows, cols)
    vm = pl.BlockSpec(memory_space=pltpu.VMEM)
    anyspace = pl.BlockSpec(memory_space=pl.ANY)
    return pl.pallas_call(
        functools.partial(exchange_kernel, rows, cols),
        out_shape=jax.ShapeDtypeStruct((1024, 2048), F32),
        in_specs=[anyspace, anyspace, vm, vm],
        out_specs=anyspace,
        scratch_shapes=[
            pltpu.VMEM((2, 512, 1024), F32),
            pltpu.VMEM((2, 512, 1024), F32),
            pltpu.VMEM((2, 512, 1024), F32),
            pltpu.VMEM((1024, 2048), F32),
            pltpu.SemaphoreType.DMA,
            pltpu.SemaphoreType.DMA((8,)),
            pltpu.SemaphoreType.DMA((2,)),
            pltpu.SemaphoreType.DMA,
        ],
        compiler_params=pltpu.CompilerParams(vmem_limit_bytes=60 << 20, has_side_effects=True),
    )(child_blocks, front, row_ids, col_ids)


def spread(value, axis, source):
    kept = jnp.where(lax.axis_index(axis) == source, value, 0).astype(value.dtype)
    return lax.psum(kept, axis)


def share_panel(values, root):
    return spread(values, "col", root)


def factor_panel(panel, section, my_row, row_count):
    pivot = spread(panel[:NB], "row", section)
    lower = jnp.linalg.cholesky(pivot)
    solved = lax.linalg.triangular_solve(
        lower, panel, left_side=False, lower=True, transpose_a=True
    )
    rows_local = panel.shape[0]
    block_ids = jnp.arange(rows_local, dtype=jnp.int32) // NB * row_count + my_row
    tiled = jnp.tile(lower, (rows_local // NB, 1))
    zeros = jnp.zeros_like(solved)
    picked = jnp.where((block_ids == section)[:, None], tiled, solved)
    return jnp.where((block_ids < section)[:, None], zeros, picked)


def column_rows(factor_rows, my_col, row_count, col_count):
    pieces = [
        spread(factor_rows, "row", my_col + turn * col_count)
        for turn in range(row_count // col_count)
    ]
    blocks = factor_rows.shape[0] // NB
    shaped = [piece.reshape(blocks, NB, NB) for piece in pieces]
    return jnp.stack(shaped, axis=1).reshape(-1, NB)


def outer_update(matrix, left_rows, right_rows):
    return matrix - jnp.dot(
        left_rows, right_rows.T, precision=lax.Precision.HIGHEST, preferred_element_type=jnp.float32
    )


def on_device(front, child_blocks, index_maps):
    row_blocks, block_rows, col_blocks, block_cols = front.shape
    row_count = lax.axis_size("row")
    col_count = lax.axis_size("col")
    my_row = lax.axis_index("row")
    my_col = lax.axis_index("col")
    summed = exchange(front, child_blocks, index_maps, row_count, col_count)
    panel = share_panel(summed[:, :NB], 0)
    outputs = []
    for section in range(2):
        factor_rows = factor_panel(panel, section, my_row, row_count)
        factor_cols = column_rows(factor_rows, my_col, row_count, col_count)
        summed = outer_update(summed, factor_rows, factor_cols)
        outputs.append(factor_rows)
        if section == 0:
            panel = share_panel(summed[:, :NB], 1)
    schur = summed.reshape(front.shape)
    factor = jnp.concatenate(outputs, axis=1).reshape(row_blocks, block_rows, 2 * NB)
    return (schur, factor)


def solution(mesh):
    placed = (P(None, "row", None, "col"), P(None, "row", "col"), P())
    return jax.shard_map(
        on_device,
        mesh=mesh,
        in_specs=placed,
        out_specs=(P(None, "row", None, "col"), P(None, "row", None)),
        check_vma=False,
    )
```

time: 1190 us -> 1100 us (0.924)
  Pallas kernels: 0 us -> 140 us
  local copies, waits for them, and re-layouts: 229 us -> 93 us
  blocking collectives: 53.2 us -> 0 us
  waiting for transfers between devices: 516 us -> 502 us
    pallas_call x0 -> x1, Pallas kernels: none -> 140 us  [exchange(): pl.pallas_call(functools.partial(exchange_kernel, rows, cols), out_shape=...]
    gather x6 -> x0, local copies, waits for them, and re-layouts: 60.6 us -> none  [the longest x4 40.6 us: on_device(): jnp.take(widened, row_take, axis=0)]
    all_to_all x1 -> x0, blocking collectives: 53.2 us -> none  [on_device(): lax.all_to_all(outgoing, 'row', split_axis=1, concat_axis=1, tiled=True)]
    unnamed x38 -> x22, local copies, waits for them, and re-layouts: 46.2 us -> 25.2 us
    reshape x6 -> x4, local copies, waits for them, and re-layouts: 17.1 us -> 3.17 us  [the longest x1 1.1 us: id_tables(): col_ids = lax.dynamic_index_in_dim(index_maps.reshape(2, cols, ratio, rat...]
    scatter x4 -> x0, local copies, waits for them, and re-layouts: 13.7 us -> none  [inverse_map(): inverse = jnp.full((length,), -1, jnp.int32).at[positions].set(arriving)]
    all_to_all x1 -> x0, waiting for transfers between devices: 13 us -> none  [on_device(): lax.all_to_all(lax.all_to_all(outgoing, 'row', split_axis=1, concat_axis=...]
    another operation x30 -> x29, other arithmetic: 159 us -> 158 us  [factor_panel(): lower = jnp.linalg.cholesky(pivot)]
  transfers between devices with their start and end apart: 7 -> 6, of which waited for: 7 -> 6; matrix products, arithmetic and copies ran while one was open for 4% -> 1% of each run, Pallas kernels for 0% -> 0%
where the time goes in v1:
time: 1100 us; the launch traced here: 1090 us
  waiting for transfers between devices  502 us (46%)
  other arithmetic  274 us (25%)
  Pallas kernels  140 us (13%)
  local copies, waits for them, and re-layouts  93 us (8%)
  matrix products  59 us (5%)
  between operations  20.2 us (2%)
    psum x6, waiting for transfers between devices, spread(): return lax.psum(kept, axis)  502 us
    another operation x29, other arithmetic, factor_panel(): lower = jnp.linalg.cholesky(pivot)  158 us
    pallas_call x1, Pallas kernels, exchange(): pl.pallas_call(functools.partial(exchange_kernel, rows, cols), out_shape=...  140 us
    another operation x5, other arithmetic, factor_panel(): lax.linalg.triangular_solve(lower, panel, left_side=False, lower=True, tr...  83.8 us
    dot_general x2, matrix products, outer_update(): jnp.dot(left_rows, right_rows.T, precision=lax.Precision.HIGHEST, preferr...  34.9 us
    unnamed x22, local copies, waits for them, and re-layouts  25.2 us
    another operation x27, local copies, waits for them, and re-layouts, factor_panel(): lax.linalg.triangular_solve(lower, panel, left_side=False, lower=True, tr...  22.7 us
  transfers between devices with their start and end apart: 6, of which 6 were waited for; matrix products, arithmetic and copies ran while one was open for 1% of the time, Pallas kernels for 0%

profile of v1, /device:TPU:115, one launch (start us, length us, event | category | flops | bytes accessed | tf_op | source)
XLA Modules:
  0.0 1089.4 jit_solution(8461793451426643979)
XLA Ops:
  13.0 139.9 %shard_map.50 = f32[1024,2048]{1,0:T(8,128)} custom-call(f32[2,512,1024]{2,1,0:T(8,128)} %child_ref.1, f32[2,512,4,512]{3,2,1,0:T(4,128)} %front_ref.1, s32[2,512]{1,0:T(2,128)} %fusion.73.row_ids_ref, s32[2,1024,1]{2,1,0:T(8,128)} %fusion.22.col_ids_ref), custom_call_target="tpu_custom_call" | custom-call | tf_op jit(solution)/shard_map/pallas_call | solution.py:153
  165.5 63.4 %all-reduce.10.cloned.1.call-done = f32[1024,512]{0,1:T(8,128)} async-done(((f32[1024,512]{0,1:T(8,128)}), f32[1024,512]{0,1:T(8,128)}) %all-reduce.10.cloned.1.call-update) | async-done | bytes 2097168 | tf_op jit(solution)/shard_map/psum | solution.py:174
  231.5 88.1 %all-reduce.12.cloned.1.call-done = f32[512,512]{0,1:T(8,128)} async-done(((f32[512,512]{0,1:T(8,128)}), f32[512,512]{0,1:T(8,128)}) %all-reduce.12.cloned.1.call-update) | async-done | bytes 1048592 | tf_op jit(solution)/shard_map/psum | solution.py:174
  321.5 11.7 %cholesky.286 = f32[128,128]{1,0:T(8,128)S(1)} custom-call(f32[128,128]{1,0:T(8,128)S(1)} %cholesky.426), custom_call_target="Cholesky" | custom-call | tf_op jit(solution)/shard_map/jit(cholesky)/cholesky | solution.py:183
  343.9 11.7 %cholesky.305 = f32[128,128]{1,0:T(8,128)S(1)} custom-call(f32[128,128]{1,0:T(8,128)S(1)} %cholesky.430), custom_call_target="Cholesky" | custom-call | tf_op jit(solution)/shard_map/jit(cholesky)/cholesky | solution.py:183
  355.6 10.2 custom-call.28
  366.5 11.7 %cholesky.326 = f32[128,128]{1,0:T(8,128)S(1)} custom-call(f32[128,128]{1,0:T(8,128)S(1)} %cholesky.435), custom_call_target="Cholesky" | custom-call | tf_op jit(solution)/shard_map/jit(cholesky)/cholesky | solution.py:183
  389.3 11.7 %cholesky.343 = f32[128,128]{1,0:T(8,128)S(1)} custom-call(f32[128,128]{1,0:T(8,128)S(1)} %convolution_subtract_fusion.11), custom_call_target="Cholesky" | custom-call | tf_op jit(solution)/shard_map/jit(cholesky)/cholesky | solution.py:183
  408.3 11.4 %while.4 = (s32[]{:T(128)}, f32[512,512]{1,0:T(8,128)}, s32[4,2]{0,1:T(2,128)S(1)}, f32[4,128,128]{2,1,0:T(8,128)S(1)}, s32[]{:T(128)}) while((s32[]{:T(128)}, f32[512,512]{1,0:T(8,128)}, s32[4,2]{0,1:T(2,128)S(1)}, f32[4,128,128]{2,1,0:T(8,128)S(1)}, s32[]{:T(128)}) %tuple.63), condition=%wide.while_cond, body=%wide.while_body.sunk | while | flops 2 | bytes 131189 | solution.py:184
  420.5 40.1 %custom-call.30 = f32[4,128,128]{1,2,0:T(8,128)S(1)} custom-call(f32[4,128,128]{2,1,0:T(8,128)} %copy-done.8), custom_call_target="InvertDiagBlocksLowerTriangular" | custom-call | tf_op jit(solution)/shard_map/triangular_solve/custom-call.3 | solution.py:184
  478.9 104.6 %all-reduce.20.cloned.1.call-done = (f32[2,1,512,512]{3,2,1,0:T(8,128)}, f32[2,1,512,512]{3,2,1,0:T(8,128)}) async-done(((f32[2,1,512,512]{3,2,1,0:T(8,128)}, f32[2,1,512,512]{3,2,1,0:T(8,128)}), (f32[2,1,512,512]{3,2,1,0:T(8,128)}, f32[2,1,512,512]{3,2,1,0:T(8,128)})) %all-reduce.20.cloned.1.call-update) | async-done | bytes 4194320 | tf_op jit(solution)/shard_map/psum | solution.py:174
  586.2 17.1 %convolution_subtract_fusion.1 = f32[1024,2048]{0,1:T(8,128)S(1)} fusion(f32[1024,2048]{0,1:T(8,128)} %copy.28, f32[1024,512]{0,1:T(8,128)S(1)} %get-tuple-element.49, f32[2048,512]{1,0:T(8,128)S(1)} %bitcast.128), kind=kOutput, calls=%fused_computation.8 | convolution fusion | flops 12886999040 | bytes 23068672 | tf_op jit(solution)/shard_map/dot_general | solution.py:206
  608.3 63.5 %all-reduce.14.cloned.1.call-done = f32[1024,512]{0,1:T(8,128)} async-done(((f32[1024,512]{0,1:T(8,128)}), f32[1024,512]{0,1:T(8,128)}) %all-reduce.14.cloned.1.call-update) | async-done | bytes 2097168 | tf_op jit(solution)/shard_map/psum | solution.py:174
  674.6 87.8 %all-reduce.16.cloned.1.call-done = f32[512,512]{0,1:T(8,128)} async-done(((f32[512,512]{0,1:T(8,128)}), f32[512,512]{0,1:T(8,128)}) %all-reduce.16.cloned.1.call-update) | async-done | bytes 1048592 | tf_op jit(solution)/shard_map/psum | solution.py:174
  767.5 11.7 %cholesky.358 = f32[128,128]{1,0:T(8,128)S(1)} custom-call(f32[128,128]{1,0:T(8,128)S(1)} %cholesky.439), custom_call_target="Cholesky" | custom-call | tf_op jit(solution)/shard_map/jit(cholesky)/cholesky | solution.py:183
  792.3 11.7 %cholesky.377 = f32[128,128]{1,0:T(8,128)S(1)} custom-call(f32[128,128]{1,0:T(8,128)S(1)} %cholesky.443), custom_call_target="Cholesky" | custom-call | tf_op jit(solution)/shard_map/jit(cholesky)/cholesky | solution.py:183
  816.3 11.7 %cholesky.398 = f32[128,128]{1,0:T(8,128)S(1)} custom-call(f32[128,128]{1,0:T(8,128)S(1)} %cholesky.448), custom_call_target="Cholesky" | custom-call | tf_op jit(solution)/shard_map/jit(cholesky)/cholesky | solution.py:183
  839.9 11.7 %cholesky.415 = f32[128,128]{1,0:T(8,128)S(1)} custom-call(f32[128,128]{1,0:T(8,128)S(1)} %convolution_subtract_fusion.10), custom_call_target="Cholesky" | custom-call | tf_op jit(solution)/shard_map/jit(cholesky)/cholesky | solution.py:183
  858.2 11.4 %while.5 = (s32[]{:T(128)}, f32[512,512]{1,0:T(8,128)}, s32[4,2]{0,1:T(2,128)S(1)}, f32[4,128,128]{2,1,0:T(8,128)S(1)}, s32[]{:T(128)}) while((s32[]{:T(128)}, f32[512,512]{1,0:T(8,128)}, s32[4,2]{0,1:T(2,128)S(1)}, f32[4,128,128]{2,1,0:T(8,128)S(1)}, s32[]{:T(128)}) %tuple.83), condition=%wide.while_cond.clone, body=%wide.while_body.clone.sunk | while | flops 2 | bytes 131189 | solution.py:184
  870.3 40.1 %custom-call.34 = f32[4,128,128]{1,2,0:T(8,128)S(1)} custom-call(f32[4,128,128]{2,1,0:T(8,128)} %copy-done.7), custom_call_target="InvertDiagBlocksLowerTriangular" | custom-call | tf_op jit(solution)/shard_map/triangular_solve/custom-call.3 | solution.py:184
  941.7 94.9 %all-reduce.18.cloned.1.call-done = (f32[2,1,512,512]{3,2,1,0:T(8,128)}, f32[2,1,512,512]{3,2,1,0:T(8,128)}) async-done(((f32[2,1,512,512]{3,2,1,0:T(8,128)}, f32[2,1,512,512]{3,2,1,0:T(8,128)}), (f32[2,1,512,512]{3,2,1,0:T(8,128)}, f32[2,1,512,512]{3,2,1,0:T(8,128)})) %all-reduce.18.cloned.1.call-update) | async-done | bytes 4194320 | tf_op jit(solution)/shard_map/psum | solution.py:174
  1039.5 17.8 %convolution_subtract_fusion = f32[1024,2048]{0,1:T(8,128)} fusion(f32[1024,2048]{0,1:T(8,128)} %copy-done, f32[1024,512]{0,1:T(8,128)S(1)} %copy-done.1, f32[2048,512]{1,0:T(8,128)S(1)} %bitcast.127), kind=kOutput, calls=%fused_computation.7 | convolution fusion | flops 12886999040 | bytes 23068672 | tf_op jit(solution)/shard_map/dot_general | solution.py:206
  1057.3 11.7 %reshape.213 = f32[2,512,4,512]{1,0,3,2:T(2,128)} reshape(f32[1024,2048]{0,1:T(8,128)} %convolution_subtract_fusion) | data formatting | bytes 16777216 | tf_op jit(solution)/shard_map/reshape | solution.py:227
  1069.0 13.2 %copy.35 = f32[2,512,4,512]{3,2,1,0:T(4,128)} copy(f32[2,512,4,512]{1,0,3,2:T(2,128)} %reshape.213) | data formatting | bytes 16777216
  (151 shorter events, 183.0 us)
Async XLA Ops:
  7.2 221.7 %all-reduce.10.cloned.1.call-start = ((), (), s32[]{:S(2)}) async-start(), calls=%async_computation | async-start | bytes 4194304 | tf_op jit(solution)/shard_map/psum | solution.py:174
  165.4 154.2 %all-reduce.12.cloned.1.call-start = ((), (), s32[]{:S(2)}) async-start(), calls=%async_computation.1 | async-start | bytes 2097152 | tf_op jit(solution)/shard_map/psum | solution.py:174
  231.2 352.3 %all-reduce.20.cloned.1.call-start = ((), (), s32[]{:S(2)}) async-start(), calls=%async_computation.5 | async-start | bytes 8388608 | tf_op jit(solution)/shard_map/psum | solution.py:174
  319.6 1.7 copy-start.4
  406.6 54.0 %copy-start.2 = (f32[1024,512]{0,1:T(8,128)S(1)}, f32[1024,512]{0,1:T(8,128)}, u32[]{:S(2)}) copy-start(f32[1024,512]{0,1:T(8,128)} %all-reduce.10.cloned.1.call-done) | copy-start | bytes 6291460
  419.7 0.7 copy-start.8
  478.7 193.2 %all-reduce.14.cloned.1.call-start = ((), (), s32[]{:S(2)}) async-start(), calls=%async_computation.2 | async-start | bytes 4194304 | tf_op jit(solution)/shard_map/psum | solution.py:174
  603.4 3.4 copy-start
  608.3 154.2 %all-reduce.16.cloned.1.call-start = ((), (), s32[]{:S(2)}) async-start(), calls=%async_computation.3 | async-start | bytes 2097152 | tf_op jit(solution)/shard_map/psum | solution.py:174
  674.2 362.5 %all-reduce.18.cloned.1.call-start = ((), (), s32[]{:S(2)}) async-start(), calls=%async_computation.4 | async-start | bytes 8388608 | tf_op jit(solution)/shard_map/psum | solution.py:174
  762.4 2.6 copy-start.5
  766.5 1.0 copy-start.6
  869.6 0.7 copy-start.7
  910.4 4.2 copy-start.3
  1036.6 2.9 copy-start.1
Sparse Core Ops, SparseCore 0:
  165.5 63.3 all-reduce.9
  232.7 86.8 all-reduce.11
  478.8 104.6 all-reduce.19
  608.4 63.4 all-reduce.13
  675.5 86.8 all-reduce.15
  932.4 104.1 all-reduce.17

commit v2 on v1

--- a/solution.py
+++ b/solution.py
@@ -1,4 +1,5 @@
 import functools
+
 import jax
 import jax.numpy as jnp
 from jax import lax
@@ -10,6 +11,8 @@
 MESH = pl.DeviceIdType.MESH
 BF = jnp.bfloat16
 F32 = jnp.float32
+VM = pltpu.VMEM
+HI = lax.Precision.HIGHEST
 
 
 def split3(value):
@@ -169,64 +172,445 @@
     )(child_blocks, front, row_ids, col_ids)
 
 
-def spread(value, axis, source):
-    kept = jnp.where(lax.axis_index(axis) == source, value, 0).astype(value.dtype)
-    return lax.psum(kept, axis)
-
-
-def share_panel(values, root):
-    return spread(values, "col", root)
-
-
-def factor_panel(panel, section, my_row, row_count):
-    pivot = spread(panel[:NB], "row", section)
-    lower = jnp.linalg.cholesky(pivot)
-    solved = lax.linalg.triangular_solve(
-        lower, panel, left_side=False, lower=True, transpose_a=True
-    )
-    rows_local = panel.shape[0]
-    block_ids = jnp.arange(rows_local, dtype=jnp.int32) // NB * row_count + my_row
-    tiled = jnp.tile(lower, (rows_local // NB, 1))
-    zeros = jnp.zeros_like(solved)
-    picked = jnp.where((block_ids == section)[:, None], tiled, solved)
-    return jnp.where((block_ids < section)[:, None], zeros, picked)
-
-
-def column_rows(factor_rows, my_col, row_count, col_count):
-    pieces = [
-        spread(factor_rows, "row", my_col + turn * col_count)
-        for turn in range(row_count // col_count)
-    ]
-    blocks = factor_rows.shape[0] // NB
-    shaped = [piece.reshape(blocks, NB, NB) for piece in pieces]
-    return jnp.stack(shaped, axis=1).reshape(-1, NB)
-
-
-def outer_update(matrix, left_rows, right_rows):
-    return matrix - jnp.dot(
-        left_rows, right_rows.T, precision=lax.Precision.HIGHEST, preferred_element_type=jnp.float32
-    )
-
-
-def on_device(front, child_blocks, index_maps):
-    row_blocks, block_rows, col_blocks, block_cols = front.shape
-    row_count = lax.axis_size("row")
-    col_count = lax.axis_size("col")
+def dot_nn(a,b): return lax.dot_general(a,b,(((1,),(0,)),((),())),precision=HI,preferred_element_type=F32)
+def dot_nt(a,b): return lax.dot_general(a,b,(((1,),(1,)),((),())),precision=HI,preferred_element_type=F32)
+
+def inverse_factor(block):
+    n = 128
+    lane = lax.broadcasted_iota(jnp.int32, (8, n), 1)
+    sub = lax.broadcasted_iota(jnp.int32, (8, n), 0)
+    tiles = [block[8 * i:8 * i + 8, :] for i in range(n // 8)]
+    for j in range(n):
+        at, inner = j // 8, j % 8
+        row = tiles[at][inner:inner + 1, :]
+        pivot = row[:, j:j + 1]
+        scaled = jnp.where(lane[:1] == j, 1.0, row) / pivot
+        for i in range(at, n // 8):
+            column = tiles[i][:, j:j + 1]
+            if i == at:
+                if inner == 7:
+                    continue
+                below = sub > inner
+                update = jnp.where(lane == j, 0.0, tiles[i]) - column * scaled
+                tiles[i] = jnp.where(below, update, tiles[i])
+            else:
+                tiles[i] = jnp.where(lane == j, 0.0, tiles[i]) - column * scaled
+    whole = jnp.concatenate(tiles, axis=0)
+    r = lax.broadcasted_iota(jnp.int32, (n, n), 0)
+    c = lax.broadcasted_iota(jnp.int32, (n, n), 1)
+    diag = jnp.sum(jnp.where(r == c, whole, 0.0), axis=1, keepdims=True)
+    unit = jnp.where(r > c, whole, jnp.where(r == c, 1.0, 0.0))
+    return unit * (1.0 / jnp.sqrt(diag))
+
+def factor_leading(lead, lower, inverse, work, corner, between):
+    n = 128
+    r = lax.broadcasted_iota(jnp.int32, (n, n), 0)
+    c = lax.broadcasted_iota(jnp.int32, (n, n), 1)
+    work[...] = lead[...]
+    lower[...] = jnp.zeros_like(lower)
+    inverse[...] = jnp.zeros_like(inverse)
+
+    @pl.loop(0, 8)
+    def _(j):
+        at = pl.ds(pl.multiple_of(j * n, n), n)
+        corner[...] = inverse_factor(work[at, at])
+        for s in range(8):
+            @pl.when(j == s)
+            def _():
+                at = slice(s * n, s * n + n)
+                w = corner[...]
+                lower[at, at] = jnp.where(r >= c, dot_nt(work[at, at], w), 0.0)
+                inverse[at, at] = w
+                if s < 7:
+                    p = dot_nt(work[s * n + n:, at], w)
+                    lower[s * n + n:, at] = p
+                    for k in range(s + 1, 8):
+                        o = (k - s - 1) * n
+                        work[k * n:, k * n:k * n + n] -= dot_nt(p[o:], p[o:o + n])
+                if s:
+                    done = slice(0, s * n)
+                    inverse[at, done] = -dot_nn(w, dot_nn(lower[at, done], inverse[done, done]))
+                if s in between:
+                    between[s]()
+
+
+def share_kernel(summed_ref, rows_out, cols_out, lower_out, inverse_out,
+                 rows_ref, cols_ref, lead_ref, lower, inverse, work, corner, sent, got, out_sems):
+    wait_bytes = cols_ref
     my_row = lax.axis_index("row")
     my_col = lax.axis_index("col")
-    summed = exchange(front, child_blocks, index_maps, row_count, col_count)
-    panel = share_panel(summed[:, :NB], 0)
-    outputs = []
-    for section in range(2):
-        factor_rows = factor_panel(panel, section, my_row, row_count)
-        factor_cols = column_rows(factor_rows, my_col, row_count, col_count)
-        summed = outer_update(summed, factor_rows, factor_cols)
-        outputs.append(factor_rows)
-        if section == 0:
-            panel = share_panel(summed[:, :NB], 1)
-    schur = summed.reshape(front.shape)
-    factor = jnp.concatenate(outputs, axis=1).reshape(row_blocks, block_rows, 2 * NB)
-    return (schur, factor)
+    y, z = my_row // 4, my_row % 4
+    x, core = my_col // 2, my_col % 2
+    chip = my_row * 4 + x
+
+    def remote(src, dst, phase, row, col, send_phase=None):
+        leaving = sent.at[phase if send_phase is None else send_phase]
+        pltpu.make_async_remote_copy(
+            src_ref=src, dst_ref=dst, send_sem=leaving, recv_sem=got.at[phase],
+            device_id=(row, col), device_id_type=MESH,
+        ).start()
+
+    def local(src, dst, phase):
+        pltpu.make_async_copy(src, dst, got.at[phase]).start()
+
+    def wait(sem, ref):
+        pltpu.make_async_copy(ref, ref, sem).wait()
+
+    def rows_of(ref, start, size, cols=None):
+        at = pl.ds(pl.multiple_of(start, 8), size)
+        if cols is None:
+            return ref.at[at]
+        return ref.at[at, pl.ds(cols[0], cols[1])]
+
+    def lead_piece(ref, block, m):
+        if block == 0:
+            return rows_of(ref, m * 8, 8, (0, 512))
+        if block == 1:
+            return rows_of(ref, 512 + m * 8, 8, (0, 256))
+        if block == 2:
+            return rows_of(ref, 512 + m * 8, 8, (256, 256))
+        return rows_of(ref, 512 + m * 8, 8, (512, 512))
+
+    def summed_piece(block, m):
+        if block == 1:
+            return rows_of(summed_ref, m * 8, 8, (0, 256))
+        if block == 2:
+            return rows_of(summed_ref, m * 8, 8, (256, 256))
+        return rows_of(summed_ref, m * 8, 8, (0, 512))
+
+    for owner_row, owner_col, blocks in ((0, 0, (0,)), (1, 0, (1, 2)), (1, 1, (3,))):
+        @pl.when((my_row == owner_row) & (my_col == owner_col))
+        def _():
+            for block in blocks:
+                target_core = 0 if block < 2 else 1
+
+                @pl.loop(0, 64)
+                def _(m):
+                    row, col = m // 4, (m % 4) * 2 + target_core
+                    here = (row == owner_row) & (col == owner_col)
+
+                    @pl.when(here)
+                    def _():
+                        local(summed_piece(block, m), lead_piece(lead_ref, block, m), 0)
+
+                    @pl.when(jnp.logical_not(here))
+                    def _():
+                        remote(
+                            summed_piece(block, m), lead_piece(lead_ref, block, m), 0, row, col,
+                            11 if block == 2 else 0,
+                        )
+
+    for src in range(2):
+        @pl.when(my_row == src)
+        def _():
+            for k in range(16):
+                piece = rows_of(summed_ref, k * 32, 32)
+                place = rows_of(cols_ref, src * NB + k * 32, 32)
+                if k == src:
+                    local(piece, place, 1)
+                else:
+                    remote(piece, place, 1, k, my_col)
+
+    for src in range(2):
+        @pl.when(my_col == src)
+        def _():
+            for k in range(4):
+                piece = rows_of(summed_ref, k * 256, 256, (0, 512))
+                place = rows_of(rows_ref, k * 256, 256, (src * 512, 512))
+                if k == 0:
+                    local(piece, place, 2)
+                else:
+                    remote(piece, place, 2, my_row, 2 * k + src)
+
+    @pl.when(core == 0)
+    def _():
+        wait(got.at[0], wait_bytes.at[pl.ds(0, 8), pl.ds(0, 768)])
+
+        @pl.loop(1, 64)
+        def _(t):
+            other = lax.rem(chip + t, 64)
+            for block in (0, 1):
+                remote(lead_piece(lead_ref, block, chip), lead_piece(lead_ref, block, chip), 3, other // 4, (other % 4) * 2)
+
+    @pl.when(core == 1)
+    def _():
+        wait(got.at[0], wait_bytes.at[pl.ds(0, 8), pl.ds(0, 768)])
+
+        @pl.loop(1, 64)
+        def _(t):
+            other = lax.rem(chip + t, 64)
+            for block in (2, 3):
+                remote(lead_piece(lead_ref, block, chip), lead_piece(lead_ref, block, chip), 3, other // 4, (other % 4) * 2 + 1)
+
+    wait(got.at[2], rows_of(wait_bytes, 0, 256, (0, 512)))
+    for core_is in range(2):
+        @pl.when(core == core_is)
+        def _():
+            for t in range(1, 4):
+                piece = rows_of(rows_ref, x * 256, 256, (core_is * 512, 512))
+                remote(piece, piece, 4, my_row, lax.rem(x + t, 4) * 2 + core_is)
+
+    wait(got.at[1], rows_of(wait_bytes, 0, 64, (0, 2048)))
+    for src in range(2):
+        left = rows_of(cols_ref, src * NB + my_row * 32, 32, (0, 1024))
+        right = rows_of(cols_ref, src * NB + my_row * 32, 32, (1024, 1024))
+        for t in range(1, 4):
+            remote(left, left, 5, y * 4 + lax.rem(z + t, 4), my_col)
+            remote(right, right, 6, lax.rem(y + t, 4) * 4 + z, my_col)
+
+    wait(got.at[3], rows_of(wait_bytes, 0, 504, (0, 768)))
+    for core_is in range(2):
+        @pl.when(core == core_is)
+        def _():
+            if core_is == 0:
+                pieces = [lead_ref.at[pl.ds(0, 512), pl.ds(0, 512)], lead_ref.at[pl.ds(512, 512), pl.ds(0, 256)]]
+            else:
+                pieces = [lead_ref.at[pl.ds(512, 512), pl.ds(256, 256)], lead_ref.at[pl.ds(512, 512), pl.ds(512, 512)]]
+            for piece in pieces:
+                remote(piece, piece, 7, my_row, x * 2 + 1 - core_is)
+
+    def second_step():
+        wait(got.at[5], rows_of(wait_bytes, 0, 192, (0, 1024)))
+        wait(got.at[6], rows_of(wait_bytes, 0, 192, (0, 1024)))
+        for src in range(2):
+            left = rows_of(cols_ref, src * NB + y * 128, 128, (0, 1024))
+            for t in range(1, 4):
+                remote(left, left, 8, lax.rem(y + t, 4) * 4 + z, my_col)
+            for k in range(4):
+                right = rows_of(cols_ref, src * NB + k * 128 + z * 32, 32, (1024, 1024))
+                for t in range(1, 4):
+                    remote(right, right, 9, y * 4 + lax.rem(z + t, 4), my_col)
+
+    def other_core():
+        wait(got.at[4], rows_of(wait_bytes, 0, 768, (0, 512)))
+        for core_is in range(2):
+            @pl.when(core == core_is)
+            def _():
+                piece = rows_ref.at[:, pl.ds(core_is * 512, 512)]
+                remote(piece, piece, 10, my_row, x * 2 + 1 - core_is)
+
+    wait(got.at[7], rows_of(wait_bytes, 0, 512, (0, 768)))
+    factor_leading(lead_ref, lower, inverse, work, corner, {1: second_step, 3: other_core})
+    outs = [
+        pltpu.make_async_copy(inverse, inverse_out, out_sems.at[0]),
+        pltpu.make_async_copy(rows_ref, rows_out, out_sems.at[1]),
+        pltpu.make_async_copy(cols_ref, cols_out, out_sems.at[2]),
+    ]
+    outs[0].start()
+    for src in range(2):
+        @pl.when(my_row == src)
+        def _():
+            pltpu.make_async_copy(lower.at[pl.ds(src * NB, NB)], lower_out, out_sems.at[3]).start()
+    wait(got.at[8], rows_of(wait_bytes, 0, 768, (0, 1024)))
+    wait(got.at[9], rows_of(wait_bytes, 0, 768, (0, 1024)))
+    wait(got.at[10], rows_of(wait_bytes, 0, 1024, (0, 512)))
+
+    outs[1].start()
+    outs[2].start()
+
+    @pl.when((my_row == 0) & (my_col == 0))
+    def _():
+        wait(sent.at[0], rows_of(wait_bytes, 0, 504, (0, 512)))
+
+    @pl.when((my_row == 1) & (my_col == 0))
+    def _():
+        wait(sent.at[0], rows_of(wait_bytes, 0, 504, (0, 256)))
+        wait(sent.at[11], rows_of(wait_bytes, 0, 512, (0, 256)))
+
+    @pl.when((my_row == 1) & (my_col == 1))
+    def _():
+        wait(sent.at[0], rows_of(wait_bytes, 0, 504, (0, 512)))
+
+    @pl.when(my_row < 2)
+    def _():
+        wait(sent.at[1], rows_of(wait_bytes, 0, 480, (0, 2048)))
+
+    @pl.when(my_col < 2)
+    def _():
+        wait(sent.at[2], rows_of(wait_bytes, 0, 768, (0, 512)))
+
+    wait(sent.at[3], rows_of(wait_bytes, 0, 504, (0, 768)))
+    wait(sent.at[4], rows_of(wait_bytes, 0, 768, (0, 512)))
+    wait(sent.at[5], rows_of(wait_bytes, 0, 192, (0, 1024)))
+    wait(sent.at[6], rows_of(wait_bytes, 0, 192, (0, 1024)))
+    wait(sent.at[7], rows_of(wait_bytes, 0, 512, (0, 768)))
+    wait(sent.at[8], rows_of(wait_bytes, 0, 768, (0, 1024)))
+    wait(sent.at[9], rows_of(wait_bytes, 0, 768, (0, 1024)))
+    wait(sent.at[10], rows_of(wait_bytes, 0, 1024, (0, 512)))
+    for out in outs:
+        out.wait()
+
+    @pl.when(my_row < 2)
+    def _():
+        pltpu.make_async_copy(lower.at[pl.ds(0, NB)], lower_out, out_sems.at[3]).wait()
+
+
+def share(summed):
+    anyspace = pl.BlockSpec(memory_space=pl.ANY)
+    return pl.pallas_call(
+        share_kernel,
+        out_shape=(
+            jax.ShapeDtypeStruct((1024, 1024), F32),
+            jax.ShapeDtypeStruct((1024, 2048), F32),
+            jax.ShapeDtypeStruct((512, 1024), F32),
+            jax.ShapeDtypeStruct((1024, 1024), F32),
+        ),
+        in_specs=[anyspace],
+        out_specs=[anyspace] * 4,
+        scratch_shapes=[
+            VM((1024, 1024), F32),
+            VM((1024, 2048), F32),
+            VM((1024, 1024), F32),
+            VM((1024, 1024), F32),
+            VM((1024, 1024), F32),
+            VM((1024, 1024), F32),
+            VM((128, 128), F32),
+            pltpu.SemaphoreType.DMA((12,)),
+            pltpu.SemaphoreType.DMA((12,)),
+            pltpu.SemaphoreType.DMA((4,)),
+        ],
+        compiler_params=pltpu.CompilerParams(vmem_limit_bytes=60 << 20, has_side_effects=True),
+    )(summed)
+
+
+def split2(value):
+    first = value.astype(BF)
+    return first, (value - first.astype(F32)).astype(BF)
+
+
+def product(left, right, dims):
+    parts = [(0, 0), (0, 1), (1, 0)]
+    total = None
+    for a, b in parts:
+        term = lax.dot_general(left[a], right[b], (dims, ((), ())), preferred_element_type=F32)
+        total = term if total is None else total + term
+    return total
+
+
+def update_kernel(summed_hbm, rows_hbm, cols_hbm, lower_hbm, inverse_hbm, schur_hbm, factor_hbm,
+                  summed, rows, cols, inverse, solved, inv_hi, inv_lo, sol_hi, sol_lo,
+                  col_hi, col_lo, y_hi, y_lo, in_sems, strip_sems, out_sems, factor_sems):
+    my_row = lax.axis_index("row")
+    loads = [
+        pltpu.make_async_copy(inverse_hbm, inverse, in_sems.at[0]),
+        pltpu.make_async_copy(rows_hbm, rows, in_sems.at[1]),
+    ]
+    for load in loads:
+        load.start()
+
+    def strip_loads(q):
+        at = pl.ds(q * NB, NB)
+        return [
+            pltpu.make_async_copy(cols_hbm.at[:, at], cols.at[:, at], strip_sems.at[2 * q]),
+            pltpu.make_async_copy(summed_hbm.at[:, at], summed.at[:, at], strip_sems.at[2 * q + 1]),
+        ]
+
+    for q in range(4):
+        for load in strip_loads(q):
+            load.start()
+    for load in loads:
+        load.wait()
+
+    for n in range(4):
+        at = slice(n * 256, n * 256 + 256)
+        inv_hi[at, :], inv_lo[at, :] = split2(inverse[at, :])
+
+    @pl.loop(0, 4)
+    def _(m):
+        at = pl.ds(pl.multiple_of(m * 256, 256), 256)
+        left = split2(rows[at, :])
+        for n in range(4):
+            past = slice(0, n * 256 + 256)
+            here = slice(n * 256, n * 256 + 256)
+            solved[at, here] = product(
+                [part[:, past] for part in left], (inv_hi[here, past], inv_lo[here, past]), ((1,), (1,))
+            )
+
+    @pl.when(my_row < 2)
+    def _():
+        load = pltpu.make_async_copy(lower_hbm, solved.at[pl.ds(0, NB)], in_sems.at[2])
+        load.start()
+        load.wait()
+
+    stores = [
+        pltpu.make_async_copy(solved.at[pl.ds(b * NB, NB)], factor_hbm.at[b], factor_sems.at[b])
+        for b in range(2)
+    ]
+    for store in stores:
+        store.start()
+    for n in range(4):
+        at = slice(n * 256, n * 256 + 256)
+        sol_hi[at, :], sol_lo[at, :] = split2(solved[at, :])
+
+    for q in range(4):
+        strip = slice(q * NB, q * NB + NB)
+        for load in strip_loads(q):
+            load.wait()
+        for n in range(4):
+            at = slice(n * 256, n * 256 + 256)
+            col_hi[at, :], col_lo[at, :] = split2(cols[at, strip])
+        for n in range(4):
+            past = slice(0, n * 256 + 256)
+            here = slice(n * 256, n * 256 + 256)
+            value = product(
+                (inv_hi[here, past], inv_lo[here, past]), (col_hi[past, :], col_lo[past, :]), ((1,), (0,))
+            )
+            y_hi[here, :], y_lo[here, :] = split2(value)
+
+        @pl.loop(0, 4)
+        def _(m):
+            at = pl.ds(pl.multiple_of(m * 256, 256), 256)
+            summed[at, strip] -= product(
+                (sol_hi[at, :], sol_lo[at, :]), (y_hi[...], y_lo[...]), ((1,), (0,))
+            )
+
+        for b in range(2):
+            store = pltpu.make_async_copy(
+                summed.at[pl.ds(b * NB, NB), pl.ds(q * NB, NB)], schur_hbm.at[b, :, q, :], out_sems.at[2 * q + b]
+            )
+            store.start()
+            stores.append(store)
+    for store in stores:
+        store.wait()
+
+
+def update(summed, rows, cols, lower, inverse):
+    anyspace = pl.BlockSpec(memory_space=pl.ANY)
+    return pl.pallas_call(
+        update_kernel,
+        out_shape=(
+            jax.ShapeDtypeStruct((2, NB, 4, NB), F32),
+            jax.ShapeDtypeStruct((2, NB, 2 * NB), F32),
+        ),
+        in_specs=[anyspace] * 5,
+        out_specs=[anyspace] * 2,
+        scratch_shapes=[
+            VM((1024, 2048), F32),
+            VM((1024, 1024), F32),
+            VM((1024, 2048), F32),
+            VM((1024, 1024), F32),
+            VM((1024, 1024), F32),
+            VM((1024, 1024), BF),
+            VM((1024, 1024), BF),
+            VM((1024, 1024), BF),
+            VM((1024, 1024), BF),
+            VM((1024, NB), BF),
+            VM((1024, NB), BF),
+            VM((1024, NB), BF),
+            VM((1024, NB), BF),
+            pltpu.SemaphoreType.DMA((3,)),
+            pltpu.SemaphoreType.DMA((8,)),
+            pltpu.SemaphoreType.DMA((8,)),
+            pltpu.SemaphoreType.DMA((2,)),
+        ],
+        compiler_params=pltpu.CompilerParams(vmem_limit_bytes=60 << 20),
+    )(summed, rows, cols, lower, inverse)
+
+
+def on_device(front, child_blocks, index_maps):
+    summed = exchange(front, child_blocks, index_maps, lax.axis_size("row"), lax.axis_size("col"))
+    rows, cols, lower, inverse = share(summed)
+    return update(summed, rows, cols, lower, inverse)
 
 
 def solution(mesh):

time: 1100 us -> 414 us (0.38)
  waiting for transfers between devices: 502 us -> 0 us
  other arithmetic: 274 us -> 2.5 us
  Pallas kernels: 140 us -> 401 us
  local copies, waits for them, and re-layouts: 93 us -> 3.22 us
  matrix products: 59 us -> 0 us
  between operations: 20.2 us -> 1.1 us
    psum x6 -> x0, waiting for transfers between devices: 502 us -> none  [spread(): return lax.psum(kept, axis)]
    pallas_call x0 -> x2, Pallas kernels: none -> 261 us  [the longest x1 221 us: share(): pl.pallas_call(share_kernel, out_shape=(jax.ShapeDtypeStruct((1024, 1024)...]
    another operation x36 -> x0, other arithmetic: 247 us -> none  [the longest x29 158 us: factor_panel(): lower = jnp.linalg.cholesky(pivot)]
    another operation x41 -> x0, local copies, waits for them, and re-layouts: 36 us -> none  [the longest x27 22.7 us: factor_panel(): lax.linalg.triangular_solve(lower, panel, left_side=False, lower=True, tr...]
    dot_general x2 -> x0, matrix products: 34.9 us -> none  [outer_update(): jnp.dot(left_rows, right_rows.T, precision=lax.Precision.HIGHEST, preferr...]
    unnamed x22 -> x0, local copies, waits for them, and re-layouts: 25.2 us -> none
    another operation x26 -> x0, matrix products: 24.1 us -> none  [the longest x14 16.7 us: factor_panel(): lax.linalg.triangular_solve(lower, panel, left_side=False, lower=True, tr...]
    select_n x8 -> x0, other arithmetic: 18.2 us -> none  [spread(): jnp.where(lax.axis_index(axis) == source, value, 0).astype(value.dtype)]
  transfers between devices with their start and end apart: 6 -> 0, of which waited for: 6 -> 0; matrix products, arithmetic and copies ran while one was open for 1% -> 0% of each run, Pallas kernels for 0% -> 0%
where the time goes in v2:
time: 414 us; the launch traced here: 408 us
  Pallas kernels  401 us (97%)
    pallas_call x1, Pallas kernels, share(): pl.pallas_call(share_kernel, out_shape=(jax.ShapeDtypeStruct((1024, 1024)...  221 us
    pallas_call x1, Pallas kernels, exchange(): pl.pallas_call(functools.partial(exchange_kernel, rows, cols), out_shape=...  140 us
    pallas_call x1, Pallas kernels, update(): pl.pallas_call(update_kernel, out_shape=(jax.ShapeDtypeStruct((2, NB, 4,...  39.7 us

profile of v2, /device:TPU:115, one launch (start us, length us, event | category | flops | bytes accessed | tf_op | source)
XLA Modules:
  0.0 407.6 jit_solution(830458634337916373)
XLA Ops:
  0.6 1.0 reshape.129
  1.7 1.0 reshape.127
  2.7 0.1 reshape.128
  2.8 0.6 fusion.5.row_ids_ref
  3.4 1.1 reshape.131
  4.5 1.9 fusion.2.col_ids_ref
  6.4 139.9 %shard_map.50.summed_ref.summed_hbm = f32[1024,2048]{1,0:T(8,128)} custom-call(f32[2,512,1024]{2,1,0:T(8,128)} %child_ref.1, f32[2,512,4,512]{3,2,1,0:T(4,128)} %front_ref.1, s32[2,512]{1,0:T(2,128)} %fusion.5.row_ids_ref, s32[2,1024,1]{2,1,0:T(8,128)} %fusion.2.col_ids_ref), custom_call_target="tpu_custom_call" | custom-call | tf_op jit(solution)/shard_map/pallas_call | solution.py:156
  146.3 221.1 %shard_map.51 = (f32[1024,1024]{1,0:T(8,128)}, f32[1024,2048]{1,0:T(8,128)}, f32[512,1024]{1,0:T(8,128)}, f32[1024,1024]{1,0:T(8,128)}) custom-call(f32[1024,2048]{1,0:T(8,128)} %shard_map.50.summed_ref.summed_hbm), custom_call_target="tpu_custom_call" | custom-call | tf_op jit(solution)/shard_map/pallas_call | solution.py:450
  367.5 39.7 %shard_map.52 = (f32[2,512,4,512]{3,2,1,0:T(4,128)}, f32[2,512,1024]{2,1,0:T(8,128)}) custom-call(f32[1024,2048]{1,0:T(8,128)} %shard_map.50.summed_ref.summed_hbm, f32[1024,1024]{1,0:T(8,128)} %get-tuple-element.6.rows_hbm, f32[1024,2048]{1,0:T(8,128)} %get-tuple-element.7.cols_hbm, f32[512,1024]{1,0:T(8,128)} %get-tuple-element.8.lower_hbm, ...), custom_call_target="tpu_custom_call" | custom-call | tf_op jit(solution)/shard_map/pallas_call | solution.py:579
  (2 shorter events, 0.1 us)
